TPU v7x, 32 devices: a whole 2x2x4 slice. The times are simulated.
32 devices in a mesh: groups: 2 (over y), feat: 4 (over z), layer: 2 (over x), tok: 2 (over core).
Axes of the slice: x: 2, y: 2, z: 4, core: 2. Of those that a mesh axis runs over, the one named last changes fastest.
Arguments:
- residual_in: float32 [256, 2, 1792], P('groups', 'tok', 'feat'), parts along dimension 0, may hold values from -6 to 6
- attn_scale: float32 [2, 256], P('layer', 'groups'), parts along dimension 1, may hold values from 0.4 to 2.5
- mlp_scale: float32 [2, 256], P('layer', 'groups'), parts along dimension 1, may hold values from 0.4 to 2.5
- patterns: bfloat16 [2, 8, 4, 64, 64], P('layer', None, 'groups'), parts along dimension 2, may hold values from 0.0029907227 to 0.059814453
- lengths: int32 [4], P('groups'), parts along dimension 0, may hold values from 16 to 64
- value_proj: bfloat16 [2, 2, 1792, 1024], P('layer', 'tok', None, 'feat'), may hold values from -0.09375 to 0.09375
- out_proj: bfloat16 [2, 4, 256, 2, 2, 1792], P('layer', None, None, None, 'tok', 'feat'), may hold values from -0.125 to 0.125
- enc_weight: bfloat16 [2, 2, 1792, 512], P('layer', 'tok', None, 'feat'), may hold values from -0.09375 to 0.09375
- enc_bias: float32 [2, 512], P('layer', 'feat'), may hold values from -3 to 3
- dec_weight: bfloat16 [2, 2, 512, 2, 1792], P('layer', None, None, 'tok', 'feat'), may hold values from -0.25 to 0.25
- errors: float32 [2, 256, 2, 1792], P('layer', 'groups', 'tok', 'feat'), parts along dimension 1, may hold values from -4 to 4
- clamp_mode: int32 [2, 16384], P('layer', 'feat'), may hold values from 0 to 2
- clamp_index: int32 [2, 16384], P('layer', 'feat'), may hold values from 0 to 63
- clamp_values: float32 [64], replicated, may hold values from 0.25 to 3
- active_blocks: int32 [2, 4], P('layer', 'feat'), may hold values from 0 to 31
Outputs:
- residual_out: float32 [2, 256, 2, 1792], P('layer', 'groups', 'tok', 'feat'), parts along dimension 1
- features: bfloat16 [2, 256, 512], P('layer', 'groups', 'feat'), parts along dimension 1
There are 2 independent parts, one for each index of `groups`. A program takes and returns all parts, laid end to end along the dimension named above; an argument that names none is the same for every part. Nothing has to cross between parts.
Inputs may be any that keep to these rules, and one draw needn't show every extreme that they name: `clamp_mode`: 0 leaves a feature free, 1 sets it to its table value, 2 multiplies it by its table value. `lengths`: positions at or past a prompt's length are padding.
All inputs are finite; a program needn't handle non-finite values.
Results may differ from a plain program's by a relative error of at most 0.018.
Values may be sent and summed in bfloat16 or wider, within the bound.
A program may use at most 64 MiB of HBM per device.

v0:
```python
import jax
import jax.numpy as jnp
from jax import lax
from jax.sharding import PartitionSpec as P


def passed_along(value, axis, steps):
    count = lax.axis_size(axis)
    initial, last = (max(0, -steps), min(count, count - steps))
    return lax.ppermute(value, axis, [(source, source + steps) for source in range(initial, last)])


def columns(normed_rows):
    return lax.all_gather(normed_rows, "feat", axis=1, tiled=True)


def halves(partial_sum):
    return lax.psum(partial_sum, "tok")


def pick_block(lookup_table, chosen, block_len):
    shaped = lookup_table.reshape(-1, block_len)
    return lax.dynamic_slice_in_dim(shaped, chosen, 1, 0)[0]


def local(
    residual_in,
    attn_scale,
    mlp_scale,
    patterns,
    lengths,
    value_proj,
    out_proj,
    enc_weight,
    enc_bias,
    dec_weight,
    errors,
    clamp_mode,
    clamp_index,
    clamp_values,
    active_blocks,
):
    layer_count = lax.axis_size("layer")
    my_layer = lax.axis_index("layer")
    my_range = lax.axis_index("feat")
    seq_len = patterns.shape[3]
    prompt_count = patterns.shape[2]
    head_dim = out_proj.shape[2]
    per_group = out_proj.shape[3]
    kv_cols = value_proj.shape[3]
    width_cols = residual_in.shape[2]
    block_len = enc_bias.shape[1]
    total_rows = residual_in.shape[0]
    split_count = 1
    block_rows = seq_len // split_count
    micro_count = prompt_count * split_count
    section_count = layer_count + micro_count - 1
    source_rows = residual_in[:, 0, :]
    error_rows = errors[0, :, 0, :]
    value_weight = value_proj[0, 0]
    out_weight = out_proj[0].reshape(-1, width_cols)
    enc_rows = enc_weight[0, 0]
    enc_shift = enc_bias[0]
    dec_rows = dec_weight[0, :, :, 0, :]
    chosen = active_blocks[0, 0]
    modes = pick_block(clamp_mode[0], chosen, block_len)
    table_pick = pick_block(clamp_index[0], chosen, block_len)
    table_ids = jnp.arange(clamp_values.shape[0], dtype=jnp.int32)
    levels = jnp.sum(
        jnp.where(table_pick[:, None] == table_ids[None, :], clamp_values[None, :], 0.0), axis=1
    )
    group_id = my_range * kv_cols // head_dim
    group_pat = lax.dynamic_slice_in_dim(patterns[0], group_id * per_group, per_group, 0)
    positions = jnp.arange(seq_len, dtype=jnp.int32)
    scale_attn = attn_scale[0]
    scale_mlp = mlp_scale[0]

    def add_heads(piece):
        return jnp.dot(piece, out_weight, preferred_element_type=jnp.float32)

    def add_writes(piece):
        return jnp.einsum("rf,tfc->trc", piece, dec_rows, preferred_element_type=jnp.float32)

    def section(step_num, carry):
        recv_rows, links, value_cache, kept_rows, kept_feats = carry
        micro_raw = step_num - my_layer
        is_live = (micro_raw >= 0) & (micro_raw < micro_count)
        micro_num = jnp.clip(micro_raw, 0, micro_count - 1)
        prompt_num = micro_num // split_count
        block_num = micro_num % split_count
        first_row = micro_num * block_rows
        first_pos = block_num * block_rows
        start_rows = lax.dynamic_slice_in_dim(source_rows, first_row, block_rows, 0)
        rows_in = jnp.where(my_layer == 0, start_rows, recv_rows)
        row_attn = lax.dynamic_slice_in_dim(scale_attn, first_row, block_rows, 0)
        normed = (rows_in * row_attn[:, None]).astype(jnp.bfloat16)
        values = halves(
            jnp.dot(columns(normed), value_weight, preferred_element_type=jnp.float32)
        ).astype(jnp.bfloat16)
        value_cache = values
        query_pos = first_pos + jnp.arange(block_rows, dtype=jnp.int32)
        prompt_len = lax.dynamic_index_in_dim(lengths, prompt_num, 0, keepdims=False)
        keep_keys = (positions[None, :] <= query_pos[:, None]) & (positions[None, :] < prompt_len)
        block_pat = lax.dynamic_slice(
            group_pat, (0, prompt_num, first_pos, 0), (per_group, 1, block_rows, seq_len)
        )[:, 0]
        block_pat = jnp.where(keep_keys[None], block_pat, jnp.zeros_like(block_pat))
        head_out = (
            jnp.einsum("uqk,kc->qcu", block_pat, value_cache, preferred_element_type=jnp.float32)
            .astype(jnp.bfloat16)
            .reshape(block_rows, -1)
        )
        attention = add_heads(lax.all_gather(head_out, "feat", axis=1, tiled=True))
        middle = rows_in + attention
        row_mlp = lax.dynamic_slice_in_dim(scale_mlp, first_row, block_rows, 0)
        normed_mlp = (middle * row_mlp[:, None]).astype(jnp.bfloat16)
        preact = (
            halves(jnp.dot(columns(normed_mlp), enc_rows, preferred_element_type=jnp.float32))
            + enc_shift
        )
        active = jnp.maximum(preact, 0.0)
        clamped = jnp.where(modes == 1, levels, jnp.where(modes == 2, active * levels, active))
        live_rows = query_pos < prompt_len
        block_feats = jnp.where(live_rows[:, None], clamped, 0.0).astype(jnp.bfloat16)
        writes = add_writes(lax.all_gather(block_feats, "feat", axis=1, tiled=True))
        error_block = lax.dynamic_slice_in_dim(error_rows, first_row, block_rows, 0)
        acc_in = jnp.where(my_layer == 0, jnp.zeros_like(links), links)
        running = acc_in + writes
        recon = lax.dynamic_index_in_dim(running, my_layer, 0, keepdims=False)
        rows_next = middle + recon + error_block
        recv_rows, links = passed_along((rows_next, running), "layer", 1)
        old_rows = lax.dynamic_slice_in_dim(kept_rows, first_row, block_rows, 0)
        kept_rows = lax.dynamic_update_slice_in_dim(
            kept_rows, jnp.where(is_live, rows_next, old_rows), first_row, 0
        )
        old_feats = lax.dynamic_slice_in_dim(kept_feats, first_row, block_rows, 0)
        kept_feats = lax.dynamic_update_slice_in_dim(
            kept_feats, jnp.where(is_live, block_feats, old_feats), first_row, 0
        )
        return (recv_rows, links, value_cache, kept_rows, kept_feats)

    link_start = jnp.zeros((layer_count, block_rows, width_cols), jnp.float32)
    initial = (
        jnp.zeros((block_rows, width_cols), jnp.float32),
        link_start,
        jnp.zeros((seq_len, kv_cols), jnp.bfloat16),
        jnp.zeros((total_rows, width_cols), jnp.float32),
        jnp.zeros((total_rows, block_len), jnp.bfloat16),
    )
    final = lax.fori_loop(0, section_count, section, initial)
    return (final[3][None, :, None, :], final[4][None])


def solution(mesh):
    return jax.shard_map(
        local,
        mesh=mesh,
        in_specs=(
            P("groups", "tok", "feat"),
            P("layer", "groups"),
            P("layer", "groups"),
            P("layer", None, "groups", None, None),
            P("groups"),
            P("layer", "tok", None, "feat"),
            P("layer", None, None, None, "tok", "feat"),
            P("layer", "tok", None, "feat"),
            P("layer", "feat"),
            P("layer", None, None, "tok", "feat"),
            P("layer", "groups", "tok", "feat"),
            P("layer", "feat"),
            P("layer", "feat"),
            P(),
            P("layer", "feat"),
        ),
        out_specs=(P("layer", "groups", "tok", "feat"), P("layer", "groups", "feat")),
        check_vma=False,
    )
```

profile of v0, /device:TPU:7, one launch (start us, length us, event | category | flops | bytes accessed | tf_op | source)
XLA Modules:
  0.0 262.9 jit_solution(8046609144955655287)
XLA Ops:
  0.7 0.9 copy-done
  2.2 0.7 fusion.19
  3.0 0.7 select_reduce_fusion
  3.7 6.1 %copy.43 = bf16[1,4,256,2,1,448]{5,3,2,1,4,0:T(2,128)(2,1)} copy(bf16[1,4,256,2,1,448]{2,5,4,3,1,0:T(8,128)(2,1)} %param.23) | data formatting | bytes 3670016 | tf_op args[6]
  9.9 3.5 %reshape_squeeze.9 = bf16[2048,448]{1,0:T(8,128)(2,1)S(1)} reshape(bf16[1,4,256,2,1,448]{5,3,2,1,4,0:T(2,128)(2,1)} %copy.43) | data formatting | bytes 3670016 | tf_op jit(solution)/shard_map/reshape;squeeze | solution.py:61
  13.5 0.8 copy.44
  14.4 0.7 broadcast.116
  15.1 0.7 broadcast_in_dim.131
  15.9 245.2 %while.23 = (s32[]{:T(128)}, f32[64,448]{1,0:T(8,128)S(1)}, f32[2,64,448]{2,1,0:T(8,128)}, f32[128,448]{1,0:T(8,128)}, bf16[128,128]{1,0:T(8,128)(2,1)S(1)}, /*i...) while((s32[]{:T(128)}, f32[64,448]{1,0:T(8,128)S(1)}, ...), condition=%wide.region_4.5_spmd.clone.clone, body=%wide.region_1.4_spmd.clone.clone.sunk | while | flops 268976448 | bytes 11732813 | solution.py:150
  16.1 12.5 %all-gather.6 = bf16[4,448,64]{1,2,0:T(8,128)(2,1)S(1)} all-gather(bf16[1,448,64]{1,2,0:T(8,128)(2,1)S(1)} %fusion.57), channel_id=1, replica_groups=mesh['groups'=2,'feat'=4,'layer'=2,'tok'=2] {'feat'}, dimensions={0}, use_global_device_ids=true | all-gather | bytes 286720 | tf_op jit(solution)/shard_map/while/body/eval_jaxpr/all_gather | solution.py:14
  28.8 0.3 reshape.85
  29.0 1.4 fusion.58
  30.5 5.8 %psum.34 = bf16[64,256]{1,0:T(8,128)(2,1)S(1)} all-reduce(f32[64,256]{1,0:T(8,128)S(1)} %fusion.58), channel_id=1, replica_groups=mesh['groups'=2,'feat'=4,'layer'=2,'tok'=2] {'tok'}, use_global_device_ids=true, to_apply=%region_2.2 | all-reduce | flops 16384 | bytes 98304 | tf_op jit(solution)/shard_map/while/body/eval_jaxpr/psum | solution.py:18
  36.3 0.7 dynamic_slice.163
  37.0 0.7 iota_compare_fusion.4
  38.0 15.1 %all_gather.48 = bf16[64,2048]{0,1:T(8,128)(2,1)S(1)} all-gather(bf16[64,512]{0,1:T(8,128)(2,1)S(1)} %bitcast.101), channel_id=1, replica_groups=mesh['groups'=2,'feat'=4,'layer'=2,'tok'=2] {'feat'}, dimensions={1}, use_global_device_ids=true | all-gather | bytes 327680 | tf_op jit(solution)/shard_map/while/body/eval_jaxpr/all_gather | solution.py:113
  53.2 0.5 convolution_add_fusion.2
  53.8 11.0 %all-gather.7 = bf16[4,448,64]{1,2,0:T(8,128)(2,1)S(1)} all-gather(bf16[1,448,64]{1,2,0:T(8,128)(2,1)S(1)} %fusion.61), channel_id=1, replica_groups=mesh['groups'=2,'feat'=4,'layer'=2,'tok'=2] {'feat'}, dimensions={0}, use_global_device_ids=true | all-gather | bytes 286720 | tf_op jit(solution)/shard_map/while/body/eval_jaxpr/all_gather | solution.py:14
  65.0 0.3 reshape.86
  65.2 1.2 fusion.62
  66.5 8.4 %psum.35 = f32[64,128]{1,0:T(8,128)S(1)} all-reduce(f32[64,128]{1,0:T(8,128)S(1)} %fusion.62), channel_id=1, replica_groups=mesh['groups'=2,'feat'=4,'layer'=2,'tok'=2] {'tok'}, use_global_device_ids=true, to_apply=%region_3.3 | all-reduce | flops 8192 | bytes 65536 | tf_op jit(solution)/shard_map/while/body/eval_jaxpr/psum | solution.py:18
  75.0 9.7 %all_gather.49 = bf16[64,512]{1,0:T(8,128)(2,1)S(1)} all-gather(bf16[64,128]{1,0:T(8,128)(2,1)S(1)} %get-tuple-element.762), channel_id=1, replica_groups=mesh['groups'=2,'feat'=4,'layer'=2,'tok'=2] {'feat'}, dimensions={1}, use_global_device_ids=true | all-gather | bytes 81920 | tf_op jit(solution)/shard_map/while/body/eval_jaxpr/all_gather | solution.py:125
  84.7 1.6 fusion.63
  86.3 1.3 collective-permute-start.1
  87.6 1.7 select_dynamic-update-slice_fusion.5
  89.3 1.3 collective-permute-start
  90.6 6.9 %collective-permute-done = f32[64,448]{1,0:T(8,128)S(1)} collective-permute-done((f32[64,448]{1,0:T(8,128)S(1)}, f32[64,448]{1,0:T(8,128)S(1)}, u32[]{:S(2)}, u32[]{:S(2)}) %collective-permute-start) | collective-permute-done | bytes 114720 | tf_op jit(solution)/shard_map/while/body/eval_jaxpr/ppermute | solution.py:10
  97.6 11.4 %all-gather.6 = bf16[4,448,64]{1,2,0:T(8,128)(2,1)S(1)} all-gather(bf16[1,448,64]{1,2,0:T(8,128)(2,1)S(1)} %fusion.57), channel_id=1, replica_groups=mesh['groups'=2,'feat'=4,'layer'=2,'tok'=2] {'feat'}, dimensions={0}, use_global_device_ids=true | all-gather | bytes 286720 | tf_op jit(solution)/shard_map/while/body/eval_jaxpr/all_gather | solution.py:14
  109.2 0.3 reshape.85
  109.5 1.5 fusion.58
  110.9 8.8 %psum.34 = bf16[64,256]{1,0:T(8,128)(2,1)S(1)} all-reduce(f32[64,256]{1,0:T(8,128)S(1)} %fusion.58), channel_id=1, replica_groups=mesh['groups'=2,'feat'=4,'layer'=2,'tok'=2] {'tok'}, use_global_device_ids=true, to_apply=%region_2.2 | all-reduce | flops 16384 | bytes 98304 | tf_op jit(solution)/shard_map/while/body/eval_jaxpr/psum | solution.py:18
  119.7 0.7 dynamic_slice.163
  120.4 0.7 iota_compare_fusion.4
  121.3 12.9 %all_gather.48 = bf16[64,2048]{0,1:T(8,128)(2,1)S(1)} all-gather(bf16[64,512]{0,1:T(8,128)(2,1)S(1)} %bitcast.101), channel_id=1, replica_groups=mesh['groups'=2,'feat'=4,'layer'=2,'tok'=2] {'feat'}, dimensions={1}, use_global_device_ids=true | all-gather | bytes 327680 | tf_op jit(solution)/shard_map/while/body/eval_jaxpr/all_gather | solution.py:113
  134.3 0.5 convolution_add_fusion.2
  134.9 11.0 %all-gather.7 = bf16[4,448,64]{1,2,0:T(8,128)(2,1)S(1)} all-gather(bf16[1,448,64]{1,2,0:T(8,128)(2,1)S(1)} %fusion.61), channel_id=1, replica_groups=mesh['groups'=2,'feat'=4,'layer'=2,'tok'=2] {'feat'}, dimensions={0}, use_global_device_ids=true | all-gather | bytes 286720 | tf_op jit(solution)/shard_map/while/body/eval_jaxpr/all_gather | solution.py:14
  146.1 0.3 reshape.86
  146.4 1.2 fusion.62
  147.6 9.5 %psum.35 = f32[64,128]{1,0:T(8,128)S(1)} all-reduce(f32[64,128]{1,0:T(8,128)S(1)} %fusion.62), channel_id=1, replica_groups=mesh['groups'=2,'feat'=4,'layer'=2,'tok'=2] {'tok'}, use_global_device_ids=true, to_apply=%region_3.3 | all-reduce | flops 8192 | bytes 65536 | tf_op jit(solution)/shard_map/while/body/eval_jaxpr/psum | solution.py:18
  157.2 9.5 %all_gather.49 = bf16[64,512]{1,0:T(8,128)(2,1)S(1)} all-gather(bf16[64,128]{1,0:T(8,128)(2,1)S(1)} %get-tuple-element.762), channel_id=1, replica_groups=mesh['groups'=2,'feat'=4,'layer'=2,'tok'=2] {'feat'}, dimensions={1}, use_global_device_ids=true | all-gather | bytes 81920 | tf_op jit(solution)/shard_map/while/body/eval_jaxpr/all_gather | solution.py:125
  166.7 1.6 fusion.63
  168.3 1.3 collective-permute-start.1
  169.6 1.7 select_dynamic-update-slice_fusion.5
  171.3 1.3 collective-permute-start
  172.6 6.9 %collective-permute-done = f32[64,448]{1,0:T(8,128)S(1)} collective-permute-done((f32[64,448]{1,0:T(8,128)S(1)}, f32[64,448]{1,0:T(8,128)S(1)}, u32[]{:S(2)}, u32[]{:S(2)}) %collective-permute-start) | collective-permute-done | bytes 114720 | tf_op jit(solution)/shard_map/while/body/eval_jaxpr/ppermute | solution.py:10
  179.7 12.2 %all-gather.6 = bf16[4,448,64]{1,2,0:T(8,128)(2,1)S(1)} all-gather(bf16[1,448,64]{1,2,0:T(8,128)(2,1)S(1)} %fusion.57), channel_id=1, replica_groups=mesh['groups'=2,'feat'=4,'layer'=2,'tok'=2] {'feat'}, dimensions={0}, use_global_device_ids=true | all-gather | bytes 286720 | tf_op jit(solution)/shard_map/while/body/eval_jaxpr/all_gather | solution.py:14
  192.1 0.3 reshape.85
  192.4 1.5 fusion.58
  193.8 7.6 %psum.34 = bf16[64,256]{1,0:T(8,128)(2,1)S(1)} all-reduce(f32[64,256]{1,0:T(8,128)S(1)} %fusion.58), channel_id=1, replica_groups=mesh['groups'=2,'feat'=4,'layer'=2,'tok'=2] {'tok'}, use_global_device_ids=true, to_apply=%region_2.2 | all-reduce | flops 16384 | bytes 98304 | tf_op jit(solution)/shard_map/while/body/eval_jaxpr/psum | solution.py:18
  201.4 0.7 dynamic_slice.163
  202.1 0.7 iota_compare_fusion.4
  203.0 13.0 %all_gather.48 = bf16[64,2048]{0,1:T(8,128)(2,1)S(1)} all-gather(bf16[64,512]{0,1:T(8,128)(2,1)S(1)} %bitcast.101), channel_id=1, replica_groups=mesh['groups'=2,'feat'=4,'layer'=2,'tok'=2] {'feat'}, dimensions={1}, use_global_device_ids=true | all-gather | bytes 327680 | tf_op jit(solution)/shard_map/while/body/eval_jaxpr/all_gather | solution.py:113
  216.1 0.5 convolution_add_fusion.2
  216.7 10.9 %all-gather.7 = bf16[4,448,64]{1,2,0:T(8,128)(2,1)S(1)} all-gather(bf16[1,448,64]{1,2,0:T(8,128)(2,1)S(1)} %fusion.61), channel_id=1, replica_groups=mesh['groups'=2,'feat'=4,'layer'=2,'tok'=2] {'feat'}, dimensions={0}, use_global_device_ids=true | all-gather | bytes 286720 | tf_op jit(solution)/shard_map/while/body/eval_jaxpr/all_gather | solution.py:14
  227.8 0.3 reshape.86
  228.1 1.2 fusion.62
  229.3 9.3 %psum.35 = f32[64,128]{1,0:T(8,128)S(1)} all-reduce(f32[64,128]{1,0:T(8,128)S(1)} %fusion.62), channel_id=1, replica_groups=mesh['groups'=2,'feat'=4,'layer'=2,'tok'=2] {'tok'}, use_global_device_ids=true, to_apply=%region_3.3 | all-reduce | flops 8192 | bytes 65536 | tf_op jit(solution)/shard_map/while/body/eval_jaxpr/psum | solution.py:18
  238.8 9.5 %all_gather.49 = bf16[64,512]{1,0:T(8,128)(2,1)S(1)} all-gather(bf16[64,128]{1,0:T(8,128)(2,1)S(1)} %get-tuple-element.762), channel_id=1, replica_groups=mesh['groups'=2,'feat'=4,'layer'=2,'tok'=2] {'feat'}, dimensions={1}, use_global_device_ids=true | all-gather | bytes 81920 | tf_op jit(solution)/shard_map/while/body/eval_jaxpr/all_gather | solution.py:125
  248.3 1.6 fusion.63
  249.9 1.3 collective-permute-start.1
  251.2 1.7 select_dynamic-update-slice_fusion.5
  252.9 1.3 collective-permute-start
  254.2 6.9 %collective-permute-done = f32[64,448]{1,0:T(8,128)S(1)} collective-permute-done((f32[64,448]{1,0:T(8,128)S(1)}, f32[64,448]{1,0:T(8,128)S(1)}, u32[]{:S(2)}, u32[]{:S(2)}) %collective-permute-start) | collective-permute-done | bytes 114720 | tf_op jit(solution)/shard_map/while/body/eval_jaxpr/ppermute | solution.py:10
  261.1 1.8 copy.45
  (55 shorter events, 3.5 us)
Async XLA Ops:
  0.6 1.0 copy-start
  9.8 3.5 %copy-start.2 = (f32[128,1,448]{0,2,1:T(8,128)S(1)}, f32[128,1,448]{0,2,1:T(8,128)}, u32[]{:S(2)}) copy-start(f32[128,1,448]{0,2,1:T(8,128)} %param.17) | copy-start | bytes 688132
  9.8 3.7 %copy-start.3 = (f32[1,128,1,448]{1,3,2,0:T(8,128)S(1)}, f32[1,128,1,448]{1,3,2,0:T(8,128)}, u32[]{:S(2)}) copy-start(f32[1,128,1,448]{1,3,2,0:T(8,128)} %param.27) | copy-start | bytes 688132
  9.8 6.0 %copy-start.4 = (f32[1,128]{1,0:T(1,128)S(1)}, f32[1,128]{1,0:T(1,128)}, u32[]{:S(2)}) copy-start(f32[1,128]{1,0:T(1,128)} %param.25) | copy-start | bytes 1540
  9.8 6.0 %copy-start.5 = (f32[1,128]{1,0:T(1,128)S(1)}, f32[1,128]{1,0:T(1,128)}, u32[]{:S(2)}) copy-start(f32[1,128]{1,0:T(1,128)} %param.18) | copy-start | bytes 1540
  9.9 6.0 %copy-start.6 = (s32[2]{0:T(128)S(1)}, s32[2]{0:T(128)}, u32[]{:S(2)}) copy-start(s32[2]{0:T(128)} %param.21) | copy-start | bytes 28
  9.9 6.0 %copy-start.7 = (f32[1,128]{1,0:T(1,128)S(1)}, f32[1,128]{1,0:T(1,128)}, u32[]{:S(2)}) copy-start(f32[1,128]{1,0:T(1,128)} %param.19) | copy-start | bytes 1540
  86.3 11.1 %collective-permute-start.1 = (f32[2,64,448]{2,1,0:T(8,128)S(1)}, f32[2,64,448]{2,1,0:T(8,128)}, u32[]{:S(2)}, u32[]{:S(2)}) collective-permute-start(f32[2,64,448]{2,1,0:T(8,128)S(1)} %fusion.63), channel_id=1, source_target_pairs={{0,2},{1,3},{4,6},{5,7},{8,10},{9,11},{12,14},{13,15},{16,18},{17,... | collective-permute-start | bytes 688136 | tf_op jit(solution)/shard_map/while/body/eval_jaxpr/ppermute | solution.py:10
  89.3 8.2 %collective-permute-start = (f32[64,448]{1,0:T(8,128)S(1)}, f32[64,448]{1,0:T(8,128)S(1)}, u32[]{:S(2)}, u32[]{:S(2)}) collective-permute-start(f32[64,448]{1,0:T(8,128)S(1)} %get-tuple-element.763), channel_id=1, source_target_pairs={{0,2},{1,3},{4,6},{5,7},{8,10},{9,11},{12,14},{13,15},{16,18},{17,... | collective-permute-start | bytes 344072 | tf_op jit(solution)/shard_map/while/body/eval_jaxpr/ppermute | solution.py:10
  168.3 11.2 %collective-permute-start.1 = (f32[2,64,448]{2,1,0:T(8,128)S(1)}, f32[2,64,448]{2,1,0:T(8,128)}, u32[]{:S(2)}, u32[]{:S(2)}) collective-permute-start(f32[2,64,448]{2,1,0:T(8,128)S(1)} %fusion.63), channel_id=1, source_target_pairs={{0,2},{1,3},{4,6},{5,7},{8,10},{9,11},{12,14},{13,15},{16,18},{17,... | collective-permute-start | bytes 688136 | tf_op jit(solution)/shard_map/while/body/eval_jaxpr/ppermute | solution.py:10
  171.3 8.2 %collective-permute-start = (f32[64,448]{1,0:T(8,128)S(1)}, f32[64,448]{1,0:T(8,128)S(1)}, u32[]{:S(2)}, u32[]{:S(2)}) collective-permute-start(f32[64,448]{1,0:T(8,128)S(1)} %get-tuple-element.763), channel_id=1, source_target_pairs={{0,2},{1,3},{4,6},{5,7},{8,10},{9,11},{12,14},{13,15},{16,18},{17,... | collective-permute-start | bytes 344072 | tf_op jit(solution)/shard_map/while/body/eval_jaxpr/ppermute | solution.py:10
  249.9 11.2 %collective-permute-start.1 = (f32[2,64,448]{2,1,0:T(8,128)S(1)}, f32[2,64,448]{2,1,0:T(8,128)}, u32[]{:S(2)}, u32[]{:S(2)}) collective-permute-start(f32[2,64,448]{2,1,0:T(8,128)S(1)} %fusion.63), channel_id=1, source_target_pairs={{0,2},{1,3},{4,6},{5,7},{8,10},{9,11},{12,14},{13,15},{16,18},{17,... | collective-permute-start | bytes 688136 | tf_op jit(solution)/shard_map/while/body/eval_jaxpr/ppermute | solution.py:10
  252.9 8.2 %collective-permute-start = (f32[64,448]{1,0:T(8,128)S(1)}, f32[64,448]{1,0:T(8,128)S(1)}, u32[]{:S(2)}, u32[]{:S(2)}) collective-permute-start(f32[64,448]{1,0:T(8,128)S(1)} %get-tuple-element.763), channel_id=1, source_target_pairs={{0,2},{1,3},{4,6},{5,7},{8,10},{9,11},{12,14},{13,15},{16,18},{17,... | collective-permute-start | bytes 344072 | tf_op jit(solution)/shard_map/while/body/eval_jaxpr/ppermute | solution.py:10
  261.1 1.8 copy-start.1
where the time goes:
time: 266 us; the launch traced here: 263 us
  blocking collectives  188 us (71%)
  local copies, waits for them, and re-layouts  21.1 us (8%)
  waiting for transfers between devices  20.7 us (8%)
  matrix products  14.8 us (6%)
  other arithmetic  8.57 us (3%)
  starting transfers between devices  7.7 us (3%)
    all_gather x6, blocking collectives, columns(): return lax.all_gather(normed_rows, 'feat', axis=1, tiled=True)  69 us
    psum x6, blocking collectives, halves(): return lax.psum(partial_sum, 'tok')  49.4 us
    all_gather x3, blocking collectives, section(): attention = add_heads(lax.all_gather(head_out, 'feat', axis=1, tiled=True))  41 us
    all_gather x3, blocking collectives, section(): writes = add_writes(lax.all_gather(block_feats, 'feat', axis=1, tiled=True))  28.8 us
    ppermute x6, waiting for transfers between devices, passed_along(): lax.ppermute(value, axis, [(source, source + steps) for source in range(i...  20.7 us
    unnamed x19, local copies, waits for them, and re-layouts  8.06 us
    ppermute x6, starting transfers between devices, passed_along(): lax.ppermute(value, axis, [(source, source + steps) for source in range(i...  7.7 us
  transfers between devices with their start and end apart: 6, of which 3 were waited for; matrix products, arithmetic and copies ran while one was open for 2% of the time, Pallas kernels for 0%

commit v1 on v0

v1 whole, which is shorter than its diff:
```python
import functools

import jax
import jax.numpy as jnp
from jax import lax
from jax.experimental import pallas as pl
from jax.experimental.pallas import tpu as pltpu
from jax.sharding import PartitionSpec as P

F32 = jnp.float32
BF16 = jnp.bfloat16
NT = (((1,), (1,)), ((), ()))


def column(row):
    rows = row.shape[1]
    return jnp.transpose(jnp.broadcast_to(row, (128, rows)))[:, 0:1]


def kernel(
    sizes,
    lengths, table, chosen,
    scale_attn, scale_mlp, bias, mode_row, index_row,
    x_in, err_in, pat_in, wv_in, wo_in, we_in, wd_in,
    out_ref, feat_ref,
    x_t, err_t, pat, wv, wo, we, wd,
    xbuf, slots, slots2, vals, feats, part_v, part_v2, part_e, part_e2,
    next_scale, nbuf, xsend, acc_in, acc_out, att,
    local_sem, xs_send, xs_recv, ns_send, v_send, v_recv, m_send, m_recv,
    f_send, f_recv, t_send, t_recv, one_send, one_recv, a_send, a_recv,
):
    layers, feat_n, seq, prompts, head_dim, per_group, kv, width, block, rows, entries = sizes
    me_l = lax.axis_index("layer")
    me_f = lax.axis_index("feat")
    me_t = lax.axis_index("tok")
    has_next = me_l < layers - 1
    has_prev = me_l > 0
    other = 1 - me_t
    nxt = jnp.minimum(me_l + 1, layers - 1)
    prv = jnp.maximum(me_l - 1, 0)

    loads = [
        pltpu.make_async_copy(src, dst, local_sem.at[i])
        for i, (src, dst) in enumerate(
            ((x_in, x_t), (wv_in, wv), (pat_in, pat), (wo_in, wo), (we_in, we), (wd_in, wd), (err_in, err_t))
        )
    ]
    for load in loads:
        load.start()
    l_x, l_wv, l_pat, l_wo, l_we, l_wd, l_err = loads

    barrier = pltpu.get_barrier_semaphore()
    pl.semaphore_signal(barrier, inc=1, device_id={"tok": other}, device_id_type=pl.DeviceIdType.MESH)
    for j in range(1, feat_n):
        pl.semaphore_signal(
            barrier, inc=1, device_id={"feat": (me_f + j) % feat_n}, device_id_type=pl.DeviceIdType.MESH
        )

    @pl.when(has_next)
    def _():
        for s in range(feat_n):
            pl.semaphore_signal(
                barrier, inc=1, device_id={"layer": nxt, "feat": s}, device_id_type=pl.DeviceIdType.MESH
            )

    @pl.when(has_prev)
    def _():
        for s in range(feat_n):
            pl.semaphore_signal(
                barrier, inc=1, device_id={"layer": prv, "feat": s}, device_id_type=pl.DeviceIdType.MESH
            )

    def send(src, dst, ss, rs, where):
        return pltpu.make_async_remote_copy(
            src_ref=src, dst_ref=dst, send_sem=ss, recv_sem=rs, device_id=where,
            device_id_type=pl.DeviceIdType.MESH,
        )

    ids = lax.broadcasted_iota(jnp.int32, (rows, 1), 0)
    limit = jnp.zeros((rows, 1), jnp.int32)
    for p in range(prompts):
        limit = jnp.where(ids // seq == p, lengths[p], limit)
    live = ids % seq < limit
    which = jnp.zeros((1, block), jnp.int32) + chosen[0, 0]
    modes = picks = jnp.zeros((1, block), jnp.int32)
    for b in range(mode_row.shape[1] // block):
        here = which == b
        modes = jnp.where(here, mode_row[:, b * block : (b + 1) * block], modes)
        picks = jnp.where(here, index_row[:, b * block : (b + 1) * block], picks)
    levels = jnp.zeros((1, block), F32)
    for v in range(entries):
        levels = jnp.where(picks == v, table[v], levels)
    mlp_col = column(scale_mlp[...])
    shift = bias[...]

    l_x.wait()
    normed_t = x_t[...] * scale_attn[...]

    @pl.when(jnp.logical_not(has_prev))
    def _():
        slots[me_f] = jnp.transpose(normed_t).astype(BF16)

    neighbours = 1 + jnp.minimum(me_l, 1) + jnp.minimum(layers - 1 - me_l, 1)
    pl.semaphore_wait(barrier, feat_n * neighbours)

    def to_peers(ref, ss, rs):
        copies = [
            send(ref.at[me_f], ref.at[me_f], ss.at[j], rs.at[me_f], {"feat": (me_f + j) % feat_n})
            for j in range(1, feat_n)
        ]
        for copy in copies:
            copy.start()
        return copies

    def arrived(ref, ss, rs, s):
        send(ref.at[s], ref.at[s], ss.at[0], rs.at[s], {"tok": other}).wait_recv()

    def await_peer(ref, ss, rs, s):
        @pl.when(me_f != s)
        def _():
            arrived(ref, ss, rs, s)

    @pl.when(jnp.logical_not(has_prev))
    def _():
        to_peers(slots, xs_send, xs_recv)
        xbuf[...] = jnp.transpose(x_t[...])

    scale_up = send(scale_attn, next_scale, one_send.at[0], one_recv.at[0], {"layer": prv})
    x_up = send(xsend, xbuf, one_send.at[1], one_recv.at[1], {"layer": nxt})

    @pl.when(has_prev)
    def _():
        scale_up.start()

    l_wv.wait()
    acc = jnp.zeros((rows, kv), F32)
    part_v[...] = acc
    for s in range(feat_n):
        @pl.when(jnp.logical_or(has_prev, me_f != s))
        def _():
            arrived(slots, xs_send, xs_recv, s)

        part_v[...] += jnp.dot(slots[s], wv[pl.ds(s * width, width), :], preferred_element_type=F32)
    tok_v = send(part_v, part_v2, t_send.at[0], t_recv.at[0], {"tok": other})
    tok_v.start()
    tok_v.wait_recv()
    vals[me_f] = (part_v[...] + part_v2[...]).astype(BF16)
    v_copies = to_peers(vals, v_send, v_recv)

    l_pat.wait()
    l_wo.wait()
    q_ids = lax.broadcasted_iota(jnp.int32, (seq, seq), 0)
    k_ids = lax.broadcasted_iota(jnp.int32, (seq, seq), 1)
    keeps = [jnp.logical_and(k_ids <= q_ids, k_ids < lengths[p]) for p in range(prompts)]
    att[...] = jnp.zeros((rows, width), F32)
    for s in range(feat_n):
        await_peer(vals, v_send, v_recv, s)
        group = s * kv // head_dim
        d0 = s * kv % head_dim
        total = att[...]
        for u in range(per_group):
            heads = []
            for p in range(prompts):
                weights = jnp.where(keeps[p], pat[group * per_group + u, p].astype(F32), 0.0).astype(BF16)
                heads.append(
                    jnp.dot(weights, vals[s, pl.ds(p * seq, seq), :], preferred_element_type=F32).astype(BF16)
                )
            head = jnp.concatenate(heads, axis=0)
            total = total + lax.dot_general(
                head, wo[group, u, :, pl.ds(d0, kv)], NT, preferred_element_type=F32
            )
        att[...] = total

    @pl.when(has_prev)
    def _():
        x_up.wait_recv()

    middle = xbuf[...] + att[...]
    att[...] = middle
    slots2[me_f] = (middle * mlp_col).astype(BF16)
    m_copies = to_peers(slots2, m_send, m_recv)
    l_we.wait()
    part_e[...] = jnp.zeros((rows, block), F32)
    for s in range(feat_n):
        await_peer(slots2, m_send, m_recv, s)
        part_e[...] += jnp.dot(slots2[s], we[pl.ds(s * width, width), :], preferred_element_type=F32)
    tok_e = send(part_e, part_e2, t_send.at[1], t_recv.at[1], {"tok": other})
    tok_e.start()
    tok_e.wait_recv()
    preact = part_e[...] + part_e2[...] + shift
    active = jnp.maximum(preact, 0.0)
    clamped = jnp.where(modes == 1, levels, jnp.where(modes == 2, active * levels, active))
    new_feats = jnp.where(live, clamped, 0.0).astype(BF16)
    feats[me_f] = new_feats
    f_copies = to_peers(feats, f_send, f_recv)
    feat_ref[...] = new_feats

    l_err.wait()
    l_wd.wait()
    att[...] += jnp.transpose(err_t[...])

    def acc_copy(t):
        return send(acc_out.at[t], acc_in.at[t], a_send.at[t], a_recv.at[t], {"layer": nxt})

    @pl.when(has_prev)
    def _():
        for t in range(1, layers):
            @pl.when(t >= me_l)
            def _():
                acc_copy(t).wait_recv()
        att[...] += acc_in[me_l]

    for s in range(feat_n):
        await_peer(feats, f_send, f_recv, s)
        att[...] += lax.dot_general(
            feats[s], wd[me_l, :, pl.ds(s * block, block)], NT, preferred_element_type=F32
        )

    norm_up = [
        send(nbuf, slots.at[me_f], ns_send.at[s], xs_recv.at[me_f], {"layer": nxt, "feat": s})
        for s in range(feat_n)
    ]

    @pl.when(has_next)
    def _():
        send(scale_attn, next_scale, one_send.at[0], one_recv.at[0], {"layer": nxt}).wait_recv()
        after = att[...]
        nbuf[...] = (after * column(next_scale[...])).astype(BF16)
        for copy in norm_up:
            copy.start()
        xsend[...] = after
        x_up.start()
        for t in range(1, layers):
            @pl.when(t > me_l)
            def _():
                total = jnp.zeros((rows, width), F32)
                for s in range(feat_n):
                    total += lax.dot_general(
                        feats[s], wd[t, :, pl.ds(s * block, block)], NT, preferred_element_type=F32
                    )
                acc_out[t] = total

                @pl.when(has_prev)
                def _():
                    acc_out[t] += acc_in[t]

                acc_copy(t).start()

    out_ref[...] = jnp.transpose(att[...])

    @pl.when(jnp.logical_not(has_prev))
    def _():
        for j in range(1, feat_n):
            send(slots.at[me_f], slots.at[me_f], xs_send.at[j], xs_recv.at[me_f], {"tok": other}).wait_send()

    @pl.when(has_prev)
    def _():
        scale_up.wait_send()

    tok_v.wait_send()
    tok_e.wait_send()
    for copy in v_copies + m_copies + f_copies:
        copy.wait_send()

    @pl.when(has_next)
    def _():
        for copy in norm_up:
            copy.wait_send()
        x_up.wait_send()
        for t in range(1, layers):
            @pl.when(t > me_l)
            def _():
                acc_copy(t).wait_send()


def local(
    residual_in, attn_scale, mlp_scale, patterns, lengths, value_proj, out_proj, enc_weight, enc_bias,
    dec_weight, errors, clamp_mode, clamp_index, clamp_values, active_blocks,
):
    layers = lax.axis_size("layer")
    feat_n = lax.axis_size("feat")
    prompts, seq = patterns.shape[2], patterns.shape[3]
    head_dim, per_group = out_proj.shape[2], out_proj.shape[3]
    kv = value_proj.shape[3]
    rows, _, width = residual_in.shape
    block = enc_bias.shape[1]
    entries = clamp_values.shape[0]
    sizes = (layers, feat_n, seq, prompts, head_dim, per_group, kv, width, block, rows, entries)
    x_in = residual_in[:, 0, :].T
    err_in = errors[0, :, 0, :].T
    pat_in = patterns[0]
    wv_in = value_proj[0, 0]
    wo_in = jnp.transpose(out_proj[0, :, :, :, 0, :], (0, 2, 3, 1))
    we_in = enc_weight[0, 0]
    wd_in = jnp.transpose(dec_weight[0, :, :, 0, :], (0, 2, 1))
    smem = pl.BlockSpec(memory_space=pltpu.SMEM)
    vmem = pl.BlockSpec(memory_space=pltpu.VMEM)
    hbm = pl.BlockSpec(memory_space=pl.ANY)
    big = (x_in, err_in, pat_in, wv_in, wo_in, we_in, wd_in)
    dma = pltpu.SemaphoreType.DMA
    out_t, out_f = pl.pallas_call(
        functools.partial(kernel, sizes),
        out_shape=(
            jax.ShapeDtypeStruct((width, rows), F32),
            jax.ShapeDtypeStruct((rows, block), BF16),
        ),
        in_specs=[smem] * 3 + [vmem] * 5 + [hbm] * 7,
        out_specs=(vmem, vmem),
        scratch_shapes=[pltpu.VMEM(a.shape, a.dtype) for a in big]
        + [
            pltpu.VMEM((rows, width), F32),
            pltpu.VMEM((feat_n, rows, width), BF16),
            pltpu.VMEM((feat_n, rows, width), BF16),
            pltpu.VMEM((feat_n, rows, kv), BF16),
            pltpu.VMEM((feat_n, rows, block), BF16),
            pltpu.VMEM((rows, kv), F32),
            pltpu.VMEM((rows, kv), F32),
            pltpu.VMEM((rows, block), F32),
            pltpu.VMEM((rows, block), F32),
            pltpu.VMEM((1, rows), F32),
            pltpu.VMEM((rows, width), BF16),
            pltpu.VMEM((rows, width), F32),
            pltpu.VMEM((layers, rows, width), F32),
            pltpu.VMEM((layers, rows, width), F32),
            pltpu.VMEM((rows, width), F32),
            dma((7,)),
        ]
        + [dma((feat_n,))] * 9
        + [dma((2,))] * 4
        + [dma((layers,))] * 2,
        compiler_params=pltpu.CompilerParams(collective_id=0, has_side_effects=True),
    )(lengths, clamp_values, active_blocks, attn_scale, mlp_scale, enc_bias, clamp_mode, clamp_index, *big)
    return out_t.T[None, :, None, :], out_f[None]


def solution(mesh):
    return jax.shard_map(
        local,
        mesh=mesh,
        in_specs=(
            P("groups", "tok", "feat"),
            P("layer", "groups"),
            P("layer", "groups"),
            P("layer", None, "groups", None, None),
            P("groups"),
            P("layer", "tok", None, "feat"),
            P("layer", None, None, None, "tok", "feat"),
            P("layer", "tok", None, "feat"),
            P("layer", "feat"),
            P("layer", None, None, "tok", "feat"),
            P("layer", "groups", "tok", "feat"),
            P("layer", "feat"),
            P("layer", "feat"),
            P(),
            P("layer", "feat"),
        ),
        out_specs=(P("layer", "groups", "tok", "feat"), P("layer", "groups", "feat")),
        check_vma=False,
    )
```

time: 266 us -> 92.6 us (0.35)
  blocking collectives: 188 us -> 0 us
  Pallas kernels: 0 us -> 87.7 us
  waiting for transfers between devices: 20.7 us -> 0 us
  local copies, waits for them, and re-layouts: 21.1 us -> 3.02 us
  matrix products: 14.8 us -> 0 us
  other arithmetic: 8.57 us -> 0 us
  starting transfers between devices: 7.7 us -> 0 us
    all_gather x12 -> x0, blocking collectives: 139 us -> none  [the longest x6 69 us: columns(): return lax.all_gather(normed_rows, 'feat', axis=1, tiled=True)]
    pallas_call x0 -> x1, Pallas kernels: none -> 87.7 us  [local(): pl.pallas_call(functools.partial(kernel, sizes), out_shape=(jax.ShapeDtyp...]
    psum x6 -> x0, blocking collectives: 49.4 us -> none  [halves(): return lax.psum(partial_sum, 'tok')]
    ppermute x6 -> x0, waiting for transfers between devices: 20.7 us -> none  [passed_along(): lax.ppermute(value, axis, [(source, source + steps) for source in range(i...]
    dot_general x15 -> x0, matrix products: 14.8 us -> none  [the longest x3 4.84 us: add_writes(): jnp.einsum('rf,tfc->trc', piece, dec_rows, preferred_element_type=jnp.flo...]
    ppermute x6 -> x0, starting transfers between devices: 7.7 us -> none  [passed_along(): lax.ppermute(value, axis, [(source, source + steps) for source in range(i...]
    dynamic_update_slice x6 -> x0, other arithmetic: 5.26 us -> none  [the longest x3 4.98 us: section(): lax.dynamic_update_slice_in_dim(kept_rows, jnp.where(is_live, rows_next,...]
    unnamed x19 -> x2, local copies, waits for them, and re-layouts: 8.06 us -> 3.02 us
  transfers between devices with their start and end apart: 6 -> 0, of which waited for: 3 -> 0; matrix products, arithmetic and copies ran while one was open for 2% -> 0% of each run, Pallas kernels for 0% -> 0%
where the time goes in v1:
time: 92.6 us; the launch traced here: 92 us
  Pallas kernels  87.7 us (95%)
  local copies, waits for them, and re-layouts  3.02 us (3%)
  between operations  1.29 us (1%)
    pallas_call x1, Pallas kernels, local(): pl.pallas_call(functools.partial(kernel, sizes), out_shape=(jax.ShapeDtyp...  87.7 us
    unnamed x2, local copies, waits for them, and re-layouts  3.02 us

profile of v1, /device:TPU:7, one launch (start us, length us, event | category | flops | bytes accessed | tf_op | source)
XLA Modules:
  0.0 92.0 jit_solution(286917115819856609)
XLA Ops:
  1.3 87.7 %shard_map.158 = (f32[448,128]{1,0:T(8,128)}, bf16[128,128]{1,0:T(8,128)(2,1)}) custom-call(s32[2]{0:T(128)} %lengths.1, f32[64]{0:T(128)} %table.1, s32[1,1]{1,0:T(1,128)S(6)} %copy.19.chosen, f32[1,128]{1,0:T(1,128)} %scale_attn.1, f32[1,128]{1,0:T(1,128)} %scale_mlp.1, f32[1,128]{1,0:T(1,128)} %bias.1, s32[1,4096]{1,0:T(1,128)} %mode_row.1, ...), custom_call_target="tpu_custom_call" | custom-call | tf_op jit(solution)/shard_map/pallas_call | solution.py:301
  89.0 1.6 %copy.20 = f32[1,128,1,448]{1,3,2,0:T(8,128)} copy(f32[1,128,1,448]{1,3,2,0:T(8,128)} %bitcast.24) | data formatting | bytes 458752
  90.6 1.4 %copy.21 = bf16[1,128,128]{2,1,0:T(8,128)(2,1)} copy(bf16[1,128,128]{2,1,0:T(8,128)(2,1)} %bitcast.27) | data formatting | bytes 65536

commit v2 on v1

v2 whole, which is shorter than its diff:
```python
import functools

import jax
import jax.numpy as jnp
from jax import lax
from jax.experimental import pallas as pl
from jax.experimental.pallas import tpu as pltpu
from jax.sharding import PartitionSpec as P

F32 = jnp.float32
BF16 = jnp.bfloat16
NT = (((1,), (1,)), ((), ()))


def column(row):
    rows = row.shape[1]
    return jnp.transpose(jnp.broadcast_to(row, (128, rows)))[:, 0:1]


def kernel(
    sizes,
    lengths, table, chosen,
    scale_attn, scale_mlp, bias, mode_row, index_row,
    x_in, err_in, pat_in, wv_in, wo_in, we_in, wd_in,
    out_ref, feat_ref,
    x_t, err_t, pat, wv, wo, we, wd,
    xbuf, slots, vals, feats, part_v, part_v2, part_e, part_e2, e_out, e_in,
    next_scale, nbuf, xsend, acc_in, acc_out, att, err, wek, relay_in, relay_mid,
    local_sem, xs_send, xs_recv, ns_send, v_send, v_recv, m_send, m_recv, f_send, f_recv,
    t_send, t_recv, up_send, up_recv, one_send, one_recv, a_send, a_recv,
    w_send, w_recv,
):
    layers, feat_n, seq, prompts, head_dim, per_group, kv, width, block, rows, entries = sizes
    me_l = lax.axis_index("layer")
    me_f = lax.axis_index("feat")
    me_t = lax.axis_index("tok")
    has_next = me_l < layers - 1
    has_prev = me_l > 0
    is_first = jnp.logical_not(has_prev)
    other = 1 - me_t
    nxt = jnp.minimum(me_l + 1, layers - 1)
    prv = jnp.maximum(me_l - 1, 0)
    streams = range(prompts)

    loads = [
        pltpu.make_async_copy(src, dst, local_sem.at[i])
        for i, (src, dst) in enumerate(
            ((x_in, x_t), (we_in, we), (wv_in, wv), (pat_in, pat), (wo_in, wo), (wd_in, wd), (err_in, err_t))
        )
    ]
    for load in loads:
        load.start()
    l_x, l_we, l_wv, l_pat, l_wo, l_wd, l_err = loads

    barrier = pltpu.get_barrier_semaphore()
    mesh_id = pl.DeviceIdType.MESH
    pl.semaphore_signal(barrier, inc=1, device_id={"tok": other}, device_id_type=mesh_id)
    for j in range(1, feat_n):
        pl.semaphore_signal(barrier, inc=1, device_id={"feat": (me_f + j) % feat_n}, device_id_type=mesh_id)

    @pl.when(has_next)
    def _():
        for s in range(feat_n):
            pl.semaphore_signal(barrier, inc=1, device_id={"layer": nxt, "feat": s}, device_id_type=mesh_id)

    @pl.when(has_prev)
    def _():
        for s in range(feat_n):
            pl.semaphore_signal(barrier, inc=1, device_id={"layer": prv, "feat": s}, device_id_type=mesh_id)

    def send(src, dst, ss, rs, where):
        return pltpu.make_async_remote_copy(
            src_ref=src, dst_ref=dst, send_sem=ss, recv_sem=rs, device_id=where, device_id_type=mesh_id
        )

    def peer(j):
        return (me_f + j) % feat_n

    def part(p):
        return pl.ds(p * seq, seq)

    l_x.wait()
    x_rows = jnp.transpose(x_t[...])
    normed = (x_rows * column(scale_attn[...])).astype(BF16)

    @pl.when(is_first)
    def _():
        for p in streams:
            slots[p, me_f] = normed[p * seq : (p + 1) * seq]
            xbuf[p] = x_rows[p * seq : (p + 1) * seq]

    neighbours = 1 + jnp.minimum(me_l, 1) + jnp.minimum(layers - 1 - me_l, 1)
    pl.semaphore_wait(barrier, feat_n * neighbours)

    def to_peers(ref, ss, rs, p):
        copies = [
            send(ref.at[p, me_f], ref.at[p, me_f], ss.at[p, j], rs.at[p, me_f], {"feat": peer(j)})
            for j in range(1, feat_n)
        ]
        for copy in copies:
            copy.start()
        return copies

    def arrived(ref, ss, rs, p, s):
        send(ref.at[p, s], ref.at[p, s], ss.at[p, 0], rs.at[p, s], {"tok": other}).wait_recv()

    def await_peer(ref, ss, rs, p, s):
        @pl.when(me_f != s)
        def _():
            arrived(ref, ss, rs, p, s)

    @pl.when(is_first)
    def _():
        for p in streams:
            to_peers(slots, xs_send, xs_recv, p)

    scale_up = send(scale_attn, next_scale, one_send.at[0], one_recv.at[0], {"layer": prv})
    x_up = [send(xsend.at[p], xbuf.at[p], up_send.at[p], up_recv.at[p], {"layer": nxt}) for p in streams]

    @pl.when(has_prev)
    def _():
        scale_up.start()

    def we_rows(s):
        return we.at[pl.ds(pl.multiple_of(s * width, 16), width)]

    l_we.wait()
    own_rows = pltpu.make_async_copy(we_rows(me_f), wek.at[me_f], local_sem.at[7])
    own_rows.start()
    first_up = [
        send(we_rows(peer(j)), relay_in.at[peer(j)], w_send.at[0, j], w_recv.at[0, peer(j)], {"layer": nxt})
        for j in range(1, feat_n)
    ]
    across = [
        send(relay_in.at[peer(j)], relay_mid.at[me_f], w_send.at[1, j], w_recv.at[1, me_f], {"feat": peer(j)})
        for j in range(1, feat_n)
    ]
    back = [
        send(relay_mid.at[peer(j)], wek.at[peer(j)], w_send.at[2, j], w_recv.at[2, peer(j)], {"layer": prv})
        for j in range(1, feat_n)
    ]
    direct = [
        send(we_rows(peer(j)), wek.at[me_f], w_send.at[3, j], w_recv.at[2, me_f], {"feat": peer(j)})
        for j in range(1, feat_n)
    ]

    def w_arrived(ref, stage, s):
        send(ref.at[s], ref.at[s], w_send.at[stage, 0], w_recv.at[stage, s], {"tok": other}).wait_recv()

    @pl.when(is_first)
    def _():
        for copy in first_up:
            copy.start()

    @pl.when(me_l == 1)
    def _():
        for j in range(1, feat_n):
            w_arrived(relay_in, 0, peer(j))
            across[j - 1].start()
        for j in range(1, feat_n):
            w_arrived(relay_mid, 1, peer(j))
            back[j - 1].start()

    @pl.when(has_prev)
    def _():
        for copy in direct:
            copy.start()

    ids = lax.broadcasted_iota(jnp.int32, (seq, 1), 0)
    lives = [ids < lengths[p] for p in streams]
    which = jnp.zeros((1, block), jnp.int32) + chosen[0, 0]
    modes = picks = jnp.zeros((1, block), jnp.int32)
    for b in range(mode_row.shape[1] // block):
        here = which == b
        modes = jnp.where(here, mode_row[:, b * block : (b + 1) * block], modes)
        picks = jnp.where(here, index_row[:, b * block : (b + 1) * block], picks)
    levels = jnp.zeros((1, block), F32)
    for v in range(entries):
        levels = jnp.where(picks == v, table[v], levels)
    mlp_col = column(scale_mlp[...])
    shift = bias[...]
    l_err.wait()
    err[...] = jnp.transpose(err_t[...])
    l_wv.wait()
    l_pat.wait()
    l_wo.wait()
    l_wd.wait()
    own_rows.wait()

    tok_v = [send(part_v.at[p], part_v2.at[p], t_send.at[0, p], t_recv.at[0, p], {"tok": other}) for p in streams]
    tok_e = [send(part_e.at[p], part_e2.at[p], t_send.at[1, p], t_recv.at[1, p], {"tok": other}) for p in streams]
    pending = []
    for p in streams:
        total = jnp.zeros((seq, kv), F32)
        for s in range(feat_n):
            @pl.when(jnp.logical_or(has_prev, me_f != s))
            def _():
                arrived(slots, xs_send, xs_recv, p, s)

            total += jnp.dot(slots[p, s], wv[pl.ds(s * width, width), :], preferred_element_type=F32)
        part_v[p] = total
        tok_v[p].start()
        tok_v[p].wait_recv()
        vals[p, me_f] = (part_v[p] + part_v2[p]).astype(BF16)
        pending += to_peers(vals, v_send, v_recv, p)

    q_ids = lax.broadcasted_iota(jnp.int32, (seq, seq), 0)
    k_ids = lax.broadcasted_iota(jnp.int32, (seq, seq), 1)
    for p in streams:
        keep = jnp.logical_and(k_ids <= q_ids, k_ids < lengths[p])
        total = jnp.zeros((seq, width), F32)
        for s in range(feat_n):
            await_peer(vals, v_send, v_recv, p, s)
            group = s * kv // head_dim
            d0 = s * kv % head_dim
            for u in range(per_group):
                weights = jnp.where(keep, pat[group * per_group + u, p].astype(F32), 0.0).astype(BF16)
                head = jnp.dot(weights, vals[p, s], preferred_element_type=F32).astype(BF16)
                total += lax.dot_general(head, wo[group, u, :, pl.ds(d0, kv)], NT, preferred_element_type=F32)

        @pl.when(has_prev)
        def _():
            x_up[p].wait_recv()

        if p == 0:
            for s in range(feat_n):
                @pl.when(me_f != s)
                def _():
                    w_arrived(wek, 2, s)

        middle = xbuf[p] + total
        normed_mlp = (middle * mlp_col[p * seq : (p + 1) * seq]).astype(BF16)
        for j in range(1, feat_n):
            e_out[p, j] = jnp.dot(normed_mlp, wek[peer(j)], preferred_element_type=F32).astype(BF16)
            copy = send(e_out.at[p, j], e_in.at[p, me_f], m_send.at[p, j], m_recv.at[p, me_f], {"feat": peer(j)})
            copy.start()
            pending.append(copy)
        part_e[p] = jnp.dot(normed_mlp, wek[me_f], preferred_element_type=F32)
        att[part(p), :] = middle + err[part(p), :]

    for p in streams:
        for s in range(feat_n):
            @pl.when(me_f != s)
            def _():
                arrived(e_in, m_send, m_recv, p, s)
                part_e[p] += e_in[p, s].astype(F32)

        tok_e[p].start()
        tok_e[p].wait_recv()
        preact = part_e[p] + part_e2[p] + shift
        active = jnp.maximum(preact, 0.0)
        clamped = jnp.where(modes == 1, levels, jnp.where(modes == 2, active * levels, active))
        new_feats = jnp.where(lives[p], clamped, 0.0).astype(BF16)
        feats[p, me_f] = new_feats
        pending += to_peers(feats, f_send, f_recv, p)
        feat_ref[part(p), :] = new_feats

    def acc_copy(p, t):
        return send(acc_out.at[p, t], acc_in.at[p, t], a_send.at[p, t], a_recv.at[p, t], {"layer": nxt})

    def norm_up(p, s):
        return send(nbuf.at[p], slots.at[p, me_f], ns_send.at[p, s], xs_recv.at[p, me_f], {"layer": nxt, "feat": s})

    @pl.when(has_next)
    def _():
        send(scale_attn, next_scale, one_send.at[0], one_recv.at[0], {"layer": nxt}).wait_recv()

    for p in streams:
        @pl.when(has_prev)
        def _():
            for t in range(1, layers):
                @pl.when(t >= me_l)
                def _():
                    acc_copy(p, t).wait_recv()
            att[part(p), :] += acc_in[p, me_l]

        total = att[part(p), :]
        for s in range(feat_n):
            await_peer(feats, f_send, f_recv, p, s)
            total += lax.dot_general(feats[p, s], wd[me_l, :, pl.ds(s * block, block)], NT, preferred_element_type=F32)
        att[part(p), :] = total

        @pl.when(has_next)
        def _():
            after = att[part(p), :]
            nbuf[p] = (after * column(next_scale[...])[p * seq : (p + 1) * seq]).astype(BF16)
            for s in range(feat_n):
                norm_up(p, s).start()
            xsend[p] = after
            x_up[p].start()

    @pl.when(has_next)
    def _():
        for p in streams:
            for t in range(1, layers):
                @pl.when(t > me_l)
                def _():
                    total = jnp.zeros((seq, width), F32)
                    for s in range(feat_n):
                        total += lax.dot_general(
                            feats[p, s], wd[t, :, pl.ds(s * block, block)], NT, preferred_element_type=F32
                        )
                    acc_out[p, t] = total

                    @pl.when(has_prev)
                    def _():
                        acc_out[p, t] += acc_in[p, t]

                    acc_copy(p, t).start()

    out_ref[...] = jnp.transpose(att[...])

    @pl.when(is_first)
    def _():
        for p in streams:
            for j in range(1, feat_n):
                send(
                    slots.at[p, me_f], slots.at[p, me_f], xs_send.at[p, j], xs_recv.at[p, me_f], {"tok": other}
                ).wait_send()
        for copy in first_up:
            copy.wait_send()

    @pl.when(me_l == 1)
    def _():
        for copy in across + back:
            copy.wait_send()

    @pl.when(has_prev)
    def _():
        scale_up.wait_send()
        for copy in direct:
            copy.wait_send()

    for copy in tok_v + tok_e + pending:
        copy.wait_send()

    @pl.when(has_next)
    def _():
        for p in streams:
            for s in range(feat_n):
                norm_up(p, s).wait_send()
            x_up[p].wait_send()
            for t in range(1, layers):
                @pl.when(t > me_l)
                def _():
                    acc_copy(p, t).wait_send()


def local(
    residual_in, attn_scale, mlp_scale, patterns, lengths, value_proj, out_proj, enc_weight, enc_bias,
    dec_weight, errors, clamp_mode, clamp_index, clamp_values, active_blocks,
):
    layers = lax.axis_size("layer")
    feat_n = lax.axis_size("feat")
    prompts, seq = patterns.shape[2], patterns.shape[3]
    head_dim, per_group = out_proj.shape[2], out_proj.shape[3]
    kv = value_proj.shape[3]
    rows, _, width = residual_in.shape
    block = enc_bias.shape[1]
    entries = clamp_values.shape[0]
    sizes = (layers, feat_n, seq, prompts, head_dim, per_group, kv, width, block, rows, entries)
    x_in = residual_in[:, 0, :].T
    err_in = errors[0, :, 0, :].T
    pat_in = patterns[0]
    wv_in = value_proj[0, 0]
    wo_in = jnp.transpose(out_proj[0, :, :, :, 0, :], (0, 2, 3, 1))
    we_in = enc_weight[0, 0]
    wd_in = jnp.transpose(dec_weight[0, :, :, 0, :], (0, 2, 1))
    smem = pl.BlockSpec(memory_space=pltpu.SMEM)
    vmem = pl.BlockSpec(memory_space=pltpu.VMEM)
    hbm = pl.BlockSpec(memory_space=pl.ANY)
    big = (x_in, err_in, pat_in, wv_in, wo_in, we_in, wd_in)
    dma = pltpu.SemaphoreType.DMA
    out_t, out_f = pl.pallas_call(
        functools.partial(kernel, sizes),
        out_shape=(
            jax.ShapeDtypeStruct((width, rows), F32),
            jax.ShapeDtypeStruct((rows, block), BF16),
        ),
        in_specs=[smem] * 3 + [vmem] * 5 + [hbm] * 7,
        out_specs=(vmem, vmem),
        scratch_shapes=[pltpu.VMEM(a.shape, a.dtype) for a in big]
        + [
            pltpu.VMEM((prompts, seq, width), F32),
            pltpu.VMEM((prompts, feat_n, seq, width), BF16),
            pltpu.VMEM((prompts, feat_n, seq, kv), BF16),
            pltpu.VMEM((prompts, feat_n, seq, block), BF16),
            pltpu.VMEM((prompts, seq, kv), F32),
            pltpu.VMEM((prompts, seq, kv), F32),
            pltpu.VMEM((prompts, seq, block), F32),
            pltpu.VMEM((prompts, seq, block), F32),
            pltpu.VMEM((prompts, feat_n, seq, block), BF16),
            pltpu.VMEM((prompts, feat_n, seq, block), BF16),
            pltpu.VMEM((1, rows), F32),
            pltpu.VMEM((prompts, seq, width), BF16),
            pltpu.VMEM((prompts, seq, width), F32),
            pltpu.VMEM((prompts, layers, seq, width), F32),
            pltpu.VMEM((prompts, layers, seq, width), F32),
            pltpu.VMEM((rows, width), F32),
            pltpu.VMEM((rows, width), F32),
        ]
        + [pltpu.VMEM((feat_n, width, block), BF16)] * 3
        + [dma((8,))]
        + [dma((prompts, feat_n))] * 9
        + [dma((2, prompts))] * 2
        + [dma((prompts,))] * 2
        + [dma((1,))] * 2
        + [dma((prompts, layers))] * 2
        + [dma((4, feat_n)), dma((3, feat_n))],
        compiler_params=pltpu.CompilerParams(collective_id=0, has_side_effects=True),
    )(lengths, clamp_values, active_blocks, attn_scale, mlp_scale, enc_bias, clamp_mode, clamp_index, *big)
    return out_t.T[None, :, None, :], out_f[None]


def solution(mesh):
    return jax.shard_map(
        local,
        mesh=mesh,
        in_specs=(
            P("groups", "tok", "feat"),
            P("layer", "groups"),
            P("layer", "groups"),
            P("layer", None, "groups", None, None),
            P("groups"),
            P("layer", "tok", None, "feat"),
            P("layer", None, None, None, "tok", "feat"),
            P("layer", "tok", None, "feat"),
            P("layer", "feat"),
            P("layer", None, None, "tok", "feat"),
            P("layer", "groups", "tok", "feat"),
            P("layer", "feat"),
            P("layer", "feat"),
            P(),
            P("layer", "feat"),
        ),
        out_specs=(P("layer", "groups", "tok", "feat"), P("layer", "groups", "feat")),
        check_vma=False,
    )
```

time: 92.6 us -> 75.5 us (0.82)
  Pallas kernels: 87.7 us -> 70.9 us
    pallas_call x1, Pallas kernels: 87.7 us -> 70.9 us  [local(): pl.pallas_call(functools.partial(kernel, sizes), out_shape=(jax.ShapeDtyp...]
where the time goes in v2:
time: 75.5 us; the launch traced here: 75.2 us
  Pallas kernels  70.9 us (94%)
  local copies, waits for them, and re-layouts  3.02 us (4%)
  between operations  1.29 us (2%)
    pallas_call x1, Pallas kernels, local(): pl.pallas_call(functools.partial(kernel, sizes), out_shape=(jax.ShapeDtyp...  70.9 us
    unnamed x2, local copies, waits for them, and re-layouts  3.02 us

profile of v2, /device:TPU:7, one launch (start us, length us, event | category | flops | bytes accessed | tf_op | source)
XLA Modules:
  0.0 75.2 jit_solution(15215421463524101218)
XLA Ops:
  1.3 70.9 %shard_map.158 = (f32[448,128]{1,0:T(8,128)}, bf16[128,128]{1,0:T(8,128)(2,1)}) custom-call(s32[2]{0:T(128)} %lengths.1, f32[64]{0:T(128)} %table.1, s32[1,1]{1,0:T(1,128)S(6)} %copy.19.chosen, f32[1,128]{1,0:T(1,128)} %scale_attn.1, f32[1,128]{1,0:T(1,128)} %scale_mlp.1, f32[1,128]{1,0:T(1,128)} %bias.1, s32[1,4096]{1,0:T(1,128)} %mode_row.1, ...), custom_call_target="tpu_custom_call" | custom-call | tf_op jit(solution)/shard_map/pallas_call | solution.py:374
  72.2 1.6 %copy.20 = f32[1,128,1,448]{1,3,2,0:T(8,128)} copy(f32[1,128,1,448]{1,3,2,0:T(8,128)} %bitcast.24) | data formatting | bytes 458752
  73.8 1.4 %copy.21 = bf16[1,128,128]{2,1,0:T(8,128)(2,1)} copy(bf16[1,128,128]{2,1,0:T(8,128)(2,1)} %bitcast.27) | data formatting | bytes 65536

commit v3 on v2

--- a/solution.py
+++ b/solution.py
@@ -28,9 +28,10 @@
     next_scale, nbuf, xsend, acc_in, acc_out, att, err, wek, relay_in, relay_mid,
     local_sem, xs_send, xs_recv, ns_send, v_send, v_recv, m_send, m_recv, f_send, f_recv,
     t_send, t_recv, up_send, up_recv, one_send, one_recv, a_send, a_recv,
-    w_send, w_recv,
+    w_send, w_recv, b_send, b_recv,
 ):
-    layers, feat_n, seq, prompts, head_dim, per_group, kv, width, block, rows, entries = sizes
+    layers, feat_n, seq, prompts, head_dim, per_group, kv, width, block, rows, entries, shares = sizes
+    me_g = lax.axis_index("groups")
     me_l = lax.axis_index("layer")
     me_f = lax.axis_index("feat")
     me_t = lax.axis_index("tok")
@@ -89,8 +90,22 @@
             slots[p, me_f] = normed[p * seq : (p + 1) * seq]
             xbuf[p] = x_rows[p * seq : (p + 1) * seq]
 
+    for g in range(1, shares):
+        @pl.when(is_first)
+        def _():
+            pl.semaphore_signal(
+                barrier, inc=1, device_id={"groups": (me_g + g) % shares, "layer": nxt}, device_id_type=mesh_id
+            )
+
+        @pl.when(me_l == 1)
+        def _():
+            pl.semaphore_signal(
+                barrier, inc=1, device_id={"groups": (me_g + g) % shares, "layer": prv}, device_id_type=mesh_id
+            )
+
+    extra = (shares - 1) * (1 - jnp.minimum(me_l // 2, 1))
     neighbours = 1 + jnp.minimum(me_l, 1) + jnp.minimum(layers - 1 - me_l, 1)
-    pl.semaphore_wait(barrier, feat_n * neighbours)
+    pl.semaphore_wait(barrier, feat_n * neighbours + extra)
 
     def to_peers(ref, ss, rs, p):
         copies = [
@@ -127,16 +142,33 @@
     l_we.wait()
     own_rows = pltpu.make_async_copy(we_rows(me_f), wek.at[me_f], local_sem.at[7])
     own_rows.start()
+    share = width // shares
+    my_share = me_g if shares > 1 else 0
+    front = pl.ds(0, share)
     first_up = [
-        send(we_rows(peer(j)), relay_in.at[peer(j)], w_send.at[0, j], w_recv.at[0, peer(j)], {"layer": nxt})
+        send(
+            we.at[pl.ds(pl.multiple_of(peer(j) * width + my_share * share, 16), share)],
+            relay_in.at[peer(j), front], w_send.at[0, j], w_recv.at[0, peer(j)], {"layer": nxt},
+        )
         for j in range(1, feat_n)
     ]
     across = [
-        send(relay_in.at[peer(j)], relay_mid.at[me_f], w_send.at[1, j], w_recv.at[1, me_f], {"feat": peer(j)})
+        send(
+            relay_in.at[peer(j), front], relay_mid.at[me_f, front],
+            w_send.at[1, j], w_recv.at[1, me_f], {"feat": peer(j)},
+        )
         for j in range(1, feat_n)
     ]
     back = [
-        send(relay_mid.at[peer(j)], wek.at[peer(j)], w_send.at[2, j], w_recv.at[2, peer(j)], {"layer": prv})
+        [
+            send(
+                relay_mid.at[peer(j), front],
+                wek.at[peer(j), pl.ds(pl.multiple_of(my_share * share, 16), share)],
+                b_send.at[g, j], b_recv.at[my_share, peer(j)],
+                {"layer": prv, "groups": (me_g + g) % shares} if g else {"layer": prv},
+            )
+            for g in range(shares)
+        ]
         for j in range(1, feat_n)
     ]
     direct = [
@@ -145,7 +177,8 @@
     ]
 
     def w_arrived(ref, stage, s):
-        send(ref.at[s], ref.at[s], w_send.at[stage, 0], w_recv.at[stage, s], {"tok": other}).wait_recv()
+        part_ref = ref.at[s, front] if stage < 2 else ref.at[s]
+        send(part_ref, part_ref, w_send.at[stage, 0], w_recv.at[stage, s], {"tok": other}).wait_recv()
 
     @pl.when(is_first)
     def _():
@@ -159,7 +192,8 @@
             across[j - 1].start()
         for j in range(1, feat_n):
             w_arrived(relay_mid, 1, peer(j))
-            back[j - 1].start()
+            for copy in back[j - 1]:
+                copy.start()
 
     @pl.when(has_prev)
     def _():
@@ -224,9 +258,15 @@
 
         if p == 0:
             for s in range(feat_n):
-                @pl.when(me_f != s)
+                @pl.when(jnp.logical_and(has_prev, me_f != s))
                 def _():
                     w_arrived(wek, 2, s)
+
+                @pl.when(jnp.logical_and(is_first, me_f != s))
+                def _():
+                    for g in range(shares):
+                        here = wek.at[s, pl.ds(g * share, share)]
+                        send(here, here, b_send.at[0, 0], b_recv.at[g, s], {"tok": other}).wait_recv()
 
         middle = xbuf[p] + total
         normed_mlp = (middle * mlp_col[p * seq : (p + 1) * seq]).astype(BF16)
@@ -287,10 +327,11 @@
             for s in range(feat_n):
                 norm_up(p, s).start()
             xsend[p] = after
+
+    @pl.when(has_next)
+    def _():
+        for p in streams:
             x_up[p].start()
-
-    @pl.when(has_next)
-    def _():
         for p in streams:
             for t in range(1, layers):
                 @pl.when(t > me_l)
@@ -322,7 +363,7 @@
 
     @pl.when(me_l == 1)
     def _():
-        for copy in across + back:
+        for copy in sum(back, across):
             copy.wait_send()
 
     @pl.when(has_prev)
@@ -344,6 +385,17 @@
                 @pl.when(t > me_l)
                 def _():
                     acc_copy(p, t).wait_send()
+
+
+def store(x_ref, f_ref, out_ref, feat_ref, sems):
+    copies = [
+        pltpu.make_async_copy(x_ref, out_ref, sems.at[0]),
+        pltpu.make_async_copy(f_ref, feat_ref, sems.at[1]),
+    ]
+    for copy in copies:
+        copy.start()
+    for copy in copies:
+        copy.wait()
 
 
 def local(
@@ -358,7 +410,9 @@
     rows, _, width = residual_in.shape
     block = enc_bias.shape[1]
     entries = clamp_values.shape[0]
-    sizes = (layers, feat_n, seq, prompts, head_dim, per_group, kv, width, block, rows, entries)
+    groups = lax.axis_size("groups")
+    shares = groups if width % (16 * groups) == 0 else 1
+    sizes = (layers, feat_n, seq, prompts, head_dim, per_group, kv, width, block, rows, entries, shares)
     x_in = residual_in[:, 0, :].T
     err_in = errors[0, :, 0, :].T
     pat_in = patterns[0]
@@ -406,9 +460,20 @@
         + [dma((prompts,))] * 2
         + [dma((1,))] * 2
         + [dma((prompts, layers))] * 2
-        + [dma((4, feat_n)), dma((3, feat_n))],
+        + [dma((4, feat_n)), dma((3, feat_n))]
+        + [dma((shares, feat_n))] * 2,
         compiler_params=pltpu.CompilerParams(collective_id=0, has_side_effects=True),
     )(lengths, clamp_values, active_blocks, attn_scale, mlp_scale, enc_bias, clamp_mode, clamp_index, *big)
+    out_t, out_f = pl.pallas_call(
+        store,
+        out_shape=(
+            jax.ShapeDtypeStruct((width, rows), F32),
+            jax.ShapeDtypeStruct((rows, block), BF16),
+        ),
+        in_specs=[vmem, vmem],
+        out_specs=(hbm, hbm),
+        scratch_shapes=[dma((2,))],
+    )(out_t, out_f)
     return out_t.T[None, :, None, :], out_f[None]
 
 

time: 75.5 us -> 67.9 us (0.90)
  Pallas kernels: 70.9 us -> 66.4 us
  local copies, waits for them, and re-layouts: 3.02 us -> 0 us
    pallas_call x1, Pallas kernels: 70.9 us -> 64.8 us  [local(): pl.pallas_call(functools.partial(kernel, sizes), out_shape=(jax.ShapeDtyp...]
    unnamed x2 -> x0, local copies, waits for them, and re-layouts: 3.02 us -> none
    pallas_call x0 -> x1, Pallas kernels: none -> 1.65 us  [local(): pl.pallas_call(store, out_shape=(jax.ShapeDtypeStruct((width, rows), F32)...]
where the time goes in v3:
time: 67.9 us; the launch traced here: 67.7 us
  Pallas kernels  66.4 us (98%)
  between operations  1.29 us (2%)
    pallas_call x1, Pallas kernels, local(): pl.pallas_call(functools.partial(kernel, sizes), out_shape=(jax.ShapeDtyp...  64.8 us
    pallas_call x1, Pallas kernels, local(): pl.pallas_call(store, out_shape=(jax.ShapeDtypeStruct((width, rows), F32)...  1.65 us

profile of v3, /device:TPU:7, one launch (start us, length us, event | category | flops | bytes accessed | tf_op | source)
XLA Modules:
  0.0 67.7 jit_solution(8917957831525773713)
XLA Ops:
  1.3 64.8 %shard_map.158 = (f32[448,128]{1,0:T(8,128)}, bf16[128,128]{1,0:T(8,128)(2,1)}) custom-call(s32[2]{0:T(128)} %lengths.1, f32[64]{0:T(128)} %table.1, s32[1,1]{1,0:T(1,128)S(6)} %copy.17.chosen, f32[1,128]{1,0:T(1,128)} %scale_attn.1, f32[1,128]{1,0:T(1,128)} %scale_mlp.1, f32[1,128]{1,0:T(1,128)} %bias.1, s32[1,4096]{1,0:T(1,128)} %mode_row.1, ...), custom_call_target="tpu_custom_call" | custom-call | tf_op jit(solution)/shard_map/pallas_call | solution.py:428
  66.1 1.6 %shard_map.159 = (f32[448,128]{1,0:T(8,128)}, bf16[128,128]{1,0:T(8,128)(2,1)}) custom-call(f32[448,128]{1,0:T(8,128)} %get-tuple-element.6.x_ref, bf16[128,128]{1,0:T(8,128)(2,1)} %get-tuple-element.7.f_ref), custom_call_target="tpu_custom_call" | custom-call | tf_op jit(solution)/shard_map/pallas_call | solution.py:467
